TPU v7x, 32 devices: a whole 2x2x4 slice. The times are simulated.
32 devices in a mesh: ka: 8 (over z, y), col: 4 (over x, core).
Axes of the slice: x: 2, y: 2, z: 4, core: 2. Of those that a mesh axis runs over, the one named last changes fastest.
Arguments:
- amps: bfloat16 [16, 256, 192], P('ka', 'col'), may hold values from -6 to 6
- isdf_coeffs: bfloat16 [16, 2048, 256], P('ka', 'col'), may hold values from -0.375 to 0.375
- w_screen: bfloat16 [16, 2048, 2048], P(None, 'ka', 'col'), as said below
- energies: float32 [16, 256], P('ka', 'col'), may hold values from 0.5 to 3
- qsel: int32 [2], replicated, may hold values from 0 to 15
- partner: int32 [2, 16], replicated, may hold values from 0 to 15, each once within a row
Outputs:
- applied: float32 [16, 256, 192], P('ka', 'col')
Inputs may be any that keep to these rules, and one draw needn't show every extreme that they name: Each row of partner is a permutation of the 16 k points. `w_screen`: each of the 16 matrices is symmetric.
All inputs are finite; a program needn't handle non-finite values.
Results may differ from a plain program's by a relative error of at most 0.013.
Values may be sent and summed in bfloat16 or wider, within the bound.
A program may use at most 64 MiB of HBM per device.

v0:
```python
import jax
import jax.numpy as jnp
from jax import lax
from jax.sharding import PartitionSpec as P


def body(amps, isdf_coeffs, w_screen, energies, qsel, partner):
    k_local = amps.shape[0]
    vectors = amps.shape[2]
    offset_base = lax.axis_index("ka") * k_local
    owned = offset_base + jnp.arange(k_local, dtype=jnp.int32)
    wanted = jnp.take(partner, owned, axis=1).reshape(-1)
    everyone = lax.all_gather(amps, "ka", axis=0, tiled=True)
    picked = jnp.take(everyone, wanted, axis=0)
    partners = lax.all_gather(picked, "col", axis=1, tiled=True)
    partners = partners.reshape(2, k_local, partners.shape[1], vectors)
    densities = jnp.einsum(
        "kms,qkse->qmke", isdf_coeffs, partners, preferred_element_type=jnp.float32
    )
    width = densities.shape[1]
    densities = densities.astype(jnp.bfloat16).reshape(2, width, k_local * vectors)
    slabs = jnp.take(w_screen, qsel, axis=0)
    partials = jnp.einsum(
        "qrm,qmx->qrx",
        lax.all_gather(slabs, "ka", axis=1, tiled=True),
        densities,
        preferred_element_type=jnp.float32,
    )
    screened = lax.psum_scatter(
        partials.astype(jnp.bfloat16), "col", scatter_dimension=1, tiled=True
    ).astype(jnp.float32)
    screened = screened.astype(jnp.bfloat16).reshape(2, width, k_local, vectors)
    projected = jnp.einsum(
        "kms,qmke->kse", isdf_coeffs, screened, preferred_element_type=jnp.float32
    )
    summed = lax.psum_scatter(
        projected.astype(jnp.bfloat16), "col", scatter_dimension=1, tiled=True
    ).astype(jnp.float32)
    return summed + energies[:, :, None] * amps.astype(jnp.float32)


def solution(mesh):
    placed = (
        P("ka", "col", None),
        P("ka", "col", None),
        P(None, "ka", "col"),
        P("ka", "col"),
        P(),
        P(),
    )
    return jax.shard_map(
        body, mesh=mesh, in_specs=placed, out_specs=P("ka", "col", None), check_vma=False
    )
```

profile of v0, /device:TPU:0, one launch (start us, length us, event | category | flops | bytes accessed | tf_op | source)
XLA Modules:
  0.0 176.6 jit_solution(11480643661953069329)
XLA Ops:
  6.5 0.0 copy-start
  6.5 0.0 all-gather.2.cloned.1.call-start
  6.5 0.7 compare_select_fusion.4
  7.3 0.7 compare_and_fusion.2
  7.9 2.8 %gather_fusion = bf16[2,256,512]{2,1,0:T(8,128)(2,1)S(1)} fusion(bf16[16,256,512]{2,1,0:T(8,128)(2,1)} %param.8, s32[1024]{0:T(1024)S(1)} %pad_clamp_fusion.2), kind=kCustom, calls=%fused_computation | custom fusion | bytes 1048584 | tf_op jit(solution)/shard_map/jit(_take)/gather | solution.py:22
  10.7 0.9 broadcast_select_fusion
  11.6 0.0 all-gather.2.cloned.1.call-update
  11.7 0.0 reduce-scatter.2.cloned.1.call-start
  11.7 0.8 copy.53
  12.5 0.6 gather_fusion.1
  13.1 0.1 select_bitcast_fusion
  13.1 0.1 copy.54
  13.2 0.1 select_n.71
  13.3 0.1 select_n.69
  13.4 35.6 %all_gather.10 = bf16[16,64,192]{2,1,0:T(8,128)(2,1)S(1)} all-gather(bf16[2,64,192]{2,1,0:T(8,128)(2,1)} %param.6), channel_id=1, replica_groups=mesh['ka'=8,'col'=4] {'ka'}, dimensions={0}, use_global_device_ids=true | all-gather | bytes 442368 | tf_op jit(solution)/shard_map/all_gather | solution.py:13
  49.0 0.6 gather_fusion.2
  49.6 0.1 broadcast_select_fusion.1
  49.7 7.1 %all_gather.11 = bf16[4,256,192]{2,1,0:T(8,128)(2,1)S(1)} all-gather(bf16[4,64,192]{2,1,0:T(8,128)(2,1)S(1)} %broadcast_select_fusion.1), channel_id=1, replica_groups=mesh['ka'=8,'col'=4] {'col'}, dimensions={1}, use_global_device_ids=true | all-gather | bytes 491520 | tf_op jit(solution)/shard_map/all_gather | solution.py:15
  56.8 0.0 copy-done
  56.8 0.5 fusion
  57.3 0.1 copy.58
  57.4 33.2 %all-gather.2.cloned.1.call-done = bf16[2,2048,512]{2,1,0:T(8,128)(2,1)} async-done(((bf16[2,256,512]{2,1,0:T(8,128)(2,1)}), bf16[2,2048,512]{2,1,0:T(8,128)(2,1)}) %all-gather.2.cloned.1.call-update) | async-done | bytes 4194320 | tf_op jit(solution)/shard_map/all_gather | solution.py:25
  90.6 6.2 %convolution_convert_fusion = bf16[2,2048,384]{2,1,0:T(8,128)(2,1)} fusion(bf16[2,2048,512]{2,1,0:T(8,128)(2,1)} %all-gather.2.cloned.1.call-done, bf16[2,512,384]{1,2,0:T(8,128)(2,1)S(1)} %bitcast.25), kind=kOutput, calls=%fused_computation.3 | convolution fusion | flops 1612185600 | bytes 8126464 | tf_op jit(solution)/shard_map/qrm,qmx->qrx/dot_general | solution.py:23
  96.8 0.0 copy-start.3
  96.8 0.0 copy-start.1
  96.8 0.0 copy-start.2
  96.8 0.0 reduce-scatter.2.cloned.1.call-update
  96.9 0.0 all-reduce.3.cloned.1.call-start
  96.9 36.5 %reduce-scatter.2.cloned.1.call-done = bf16[2,512,384]{2,1,0:T(8,128)(2,1)} async-done(((bf16[2,2048,384]{2,1,0:T(8,128)(2,1)}), bf16[2,512,384]{2,1,0:T(8,128)(2,1)}) %reduce-scatter.2.cloned.1.call-update) | async-done | bytes 786448 | tf_op jit(solution)/shard_map/reduce_scatter | solution.py:29
  133.4 1.2 convert_reduce_fusion
  134.7 0.2 copy.60
  134.9 0.3 fusion.1
  135.1 0.9 copy.61
  136.0 0.0 all-reduce.3.cloned.1.call-update
  136.0 0.0 copy-done.3
  136.0 0.6 dynamic-slice
  137.3 31.2 %all-reduce.3.cloned.1.call-done = bf16[2,256,192]{2,0,1:T(2,128)(2,1)} async-done(((bf16[2,256,192]{2,0,1:T(2,128)(2,1)}), bf16[2,256,192]{2,0,1:T(2,128)(2,1)}) %all-reduce.3.cloned.1.call-update) | async-done | bytes 196624
  168.5 0.9 constant_dynamic-slice_fusion
  169.4 0.0 copy-done.1
  169.4 0.0 copy-done.2
  169.4 0.7 multiply_add_fusion
  (7 shorter events, 0.0 us)
Async XLA Ops:
  6.5 50.3 %copy-start = (bf16[2,512,256]{2,1,0:T(8,128)(2,1)S(1)}, bf16[2,512,256]{2,1,0:T(8,128)(2,1)}, u32[]{:S(2)}) copy-start(bf16[2,512,256]{2,1,0:T(8,128)(2,1)} %param.7) | copy-start | bytes 1572868
  6.5 84.1 %all-gather.2.cloned.1.call-start = ((), (), s32[]{:S(2)}) async-start(), calls=%async_computation.1 | async-start | bytes 4718592 | tf_op jit(solution)/shard_map/all_gather | solution.py:25
  11.7 121.7 %reduce-scatter.2.cloned.1.call-start = ((), (), s32[]{:S(2)}) async-start(), calls=%async_computation.2 | async-start | bytes 3932160 | tf_op jit(solution)/shard_map/reduce_scatter | solution.py:29
  96.8 39.2 %copy-start.3 = (u32[32]{0:T(128)S(1)}, u32[32]{0:T(128)}, u32[]{:S(2)}) copy-start(u32[32]{0:T(128)} %constant.56) | copy-start | bytes 388
  96.8 72.5 %copy-start.1 = (bf16[2,64,192]{2,1,0:T(8,128)(2,1)S(1)}, bf16[2,64,192]{2,1,0:T(8,128)(2,1)}, u32[]{:S(2)}) copy-start(bf16[2,64,192]{2,1,0:T(8,128)(2,1)} %param.6) | copy-start | bytes 147460
  96.8 72.5 %copy-start.2 = (f32[2,64]{1,0:T(2,128)S(1)}, f32[2,64]{1,0:T(2,128)}, u32[]{:S(2)}) copy-start(f32[2,64]{1,0:T(2,128)} %param.9) | copy-start | bytes 1540
  96.9 71.6 %all-reduce.3.cloned.1.call-start = ((), (), s32[]{:S(2)}) async-start(), calls=%async_computation.3 | async-start | bytes 524288
Sparse Core Ops, SparseCore 0:
  11.8 78.7 all-gather.1
  97.0 36.3 reduce-scatter.1
  136.2 32.2 all-reduce.2
where the time goes:
time: 177 us
  waiting for transfers between devices  101 us (57%)
  blocking collectives  42.7 us (24%)
  between operations  13.9 us (8%)
  local copies, waits for them, and re-layouts  7.5 us (4%)
  matrix products  6.98 us (4%)
  other arithmetic  4.51 us (3%)
    reduce_scatter x1, waiting for transfers between devices, body(): lax.psum_scatter(partials.astype(jnp.bfloat16), 'col', scatter_dimension=...  36.5 us
    all_gather x1, blocking collectives, body(): everyone = lax.all_gather(amps, 'ka', axis=0, tiled=True)  35.6 us
    all_gather x1, waiting for transfers between devices, body(): lax.all_gather(slabs, 'ka', axis=1, tiled=True)  33.2 us
    unnamed x4, waiting for transfers between devices  31.2 us
    all_gather x1, blocking collectives, body(): partners = lax.all_gather(picked, 'col', axis=1, tiled=True)  7.1 us
    dot_general x1, matrix products, body(): jnp.einsum('qrm,qmx->qrx', lax.all_gather(slabs, 'ka', axis=1, tiled=True...  6.23 us
  transfers between devices with their start and end apart: 3, of which 3 were waited for; matrix products, arithmetic and copies ran while one was open for 2% of the time, Pallas kernels for 0%

commit v1 on v0

--- a/solution.py
+++ b/solution.py
@@ -2,6 +2,32 @@
 import jax.numpy as jnp
 from jax import lax
 from jax.sharding import PartitionSpec as P
+
+
+def ring_apply(value, axis, dim, work, out_dim):
+    peers, place, width = (lax.axis_size(axis), lax.axis_index(axis), value.shape[dim])
+    right = [(i, (i + 1) % peers) for i in range(peers)]
+    left = [(b, a) for a, b in right]
+    lower, upper = (lax.ppermute(value, axis, right), lax.ppermute(value, axis, left))
+    made = work(value, place * width)
+    length = made.shape[out_dim]
+    filled = jnp.zeros(
+        (*made.shape[:out_dim], peers * length, *made.shape[out_dim + 1 :]), made.dtype
+    )
+
+    def put(filled, made, owner):
+        return lax.dynamic_update_slice_in_dim(filled, made, owner * length, axis=out_dim)
+
+    filled = put(filled, made, place)
+    for turn in range(1, peers // 2 + 1):
+        below, above = ((place - turn) % peers, (place + turn) % peers)
+        held = (lower, upper)
+        if turn < peers // 2:
+            lower, upper = (lax.ppermute(lower, axis, right), lax.ppermute(upper, axis, left))
+        filled = put(filled, work(held[0], below * width), below)
+        if 2 * turn < peers:
+            filled = put(filled, work(held[1], above * width), above)
+    return filled
 
 
 def body(amps, isdf_coeffs, w_screen, energies, qsel, partner):
@@ -20,11 +46,14 @@
     width = densities.shape[1]
     densities = densities.astype(jnp.bfloat16).reshape(2, width, k_local * vectors)
     slabs = jnp.take(w_screen, qsel, axis=0)
-    partials = jnp.einsum(
-        "qrm,qmx->qrx",
-        lax.all_gather(slabs, "ka", axis=1, tiled=True),
-        densities,
-        preferred_element_type=jnp.float32,
+    partials = ring_apply(
+        slabs,
+        "ka",
+        1,
+        lambda shard, start: jnp.einsum(
+            "qrm,qmx->qrx", shard, densities, preferred_element_type=jnp.float32
+        ),
+        1,
     )
     screened = lax.psum_scatter(
         partials.astype(jnp.bfloat16), "col", scatter_dimension=1, tiled=True

time: 177 us -> 220 us (1.24)
  starting transfers between devices: 0.09 us -> 18.5 us
  blocking collectives: 42.7 us -> 53 us
  waiting for transfers between devices: 101 us -> 111 us
  matrix products: 6.98 us -> 10.4 us
    ppermute x0 -> x7, waiting for transfers between devices: none -> 44.1 us  [the longest x3 44 us: ring_apply(): lax.ppermute(lower, axis, right)]
    all_gather x1 -> x0, waiting for transfers between devices: 33.2 us -> none  [body(): lax.all_gather(slabs, 'ka', axis=1, tiled=True)]
    ppermute x0 -> x7, starting transfers between devices: none -> 18.5 us  [the longest x2 7.15 us: ring_apply(): lax.ppermute(upper, axis, left)]
    all_gather x1, blocking collectives: 35.6 us -> 45.8 us  [body(): everyone = lax.all_gather(amps, 'ka', axis=0, tiled=True)]
    dot_general x1 -> x8, matrix products: 6.23 us -> 9.6 us  [body(): jnp.einsum('qrm,qmx->qrx', shard, densities, preferred_element_type=jnp.f...]
    unnamed x4 -> x3, waiting for transfers between devices: 31.2 us -> 31.2 us
  transfers between devices with their start and end apart: 3 -> 9, of which waited for: 3 -> 5; matrix products, arithmetic and copies ran while one was open for 2% -> 6% of each run, Pallas kernels for 0% -> 0%
where the time goes in v1:
time: 220 us
  waiting for transfers between devices  111 us (50%)
  blocking collectives  53 us (24%)
  starting transfers between devices  18.5 us (8%)
  between operations  14.2 us (6%)
  matrix products  10.4 us (5%)
  local copies, waits for them, and re-layouts  9.4 us (4%)
  other arithmetic  3.68 us (2%)
    all_gather x1, blocking collectives, body(): everyone = lax.all_gather(amps, 'ka', axis=0, tiled=True)  45.8 us
    ppermute x3, waiting for transfers between devices, ring_apply(): lax.ppermute(lower, axis, right)  44 us
    reduce_scatter x1, waiting for transfers between devices, body(): lax.psum_scatter(partials.astype(jnp.bfloat16), 'col', scatter_dimension=...  35.8 us
    unnamed x3, waiting for transfers between devices  31.2 us
    dot_general x8, matrix products, body(): jnp.einsum('qrm,qmx->qrx', shard, densities, preferred_element_type=jnp.f...  9.6 us
    all_gather x1, blocking collectives, body(): partners = lax.all_gather(picked, 'col', axis=1, tiled=True)  7.17 us
    ppermute x2, starting transfers between devices, ring_apply(): lax.ppermute(upper, axis, left)  7.15 us
    ppermute x3, starting transfers between devices, ring_apply(): lax.ppermute(lower, axis, right)  5.18 us
  transfers between devices with their start and end apart: 9, of which 5 were waited for; matrix products, arithmetic and copies ran while one was open for 6% of the time, Pallas kernels for 0%

profile of v1, /device:TPU:0, one launch (start us, length us, event | category | flops | bytes accessed | tf_op | source)
XLA Modules:
  0.0 220.2 jit_solution(1654478903644720548)
XLA Ops:
  6.5 0.0 copy-start
  6.5 0.0 reduce-scatter.2.cloned.1.call-start
  6.5 0.7 compare_select_fusion.4
  7.3 0.7 compare_and_fusion.1
  7.9 2.8 %gather_fusion = bf16[2,256,512]{2,1,0:T(8,128)(2,1)S(1)} fusion(bf16[16,256,512]{2,1,0:T(8,128)(2,1)} %param.8, s32[1024]{0:T(1024)S(1)} %pad_clamp_fusion.2), kind=kCustom, calls=%fused_computation | custom fusion | bytes 1048584 | tf_op jit(solution)/shard_map/jit(_take)/gather | solution.py:48
  10.7 0.1 broadcast_select_fusion
  10.8 3.0 %collective-permute-start = (bf16[2,256,512]{2,1,0:T(8,128)(2,1)S(1)}, bf16[2,256,512]{2,1,0:T(8,128)(2,1)S(1)}, u32[]{:S(2)}, u32[]{:S(2)}) collective-permute-start(bf16[2,256,512]{2,1,0:T(8,128)(2,1)S(1)} %broadcast_select_fusion), channel_id=1, source_target_pairs={{0,4},{4,8},{8,12},{12,16},{16,20},{20,24},{24,28},{28,0},{1,5},{5... | collective-permute-start | bytes 1572872 | tf_op jit(solution)/shard_map/ppermute | solution.py:11
  13.9 3.1 %collective-permute-start.1 = (bf16[2,256,512]{2,1,0:T(8,128)(2,1)S(1)}, bf16[2,256,512]{2,1,0:T(8,128)(2,1)S(1)}, u32[]{:S(2)}, u32[]{:S(2)}) collective-permute-start(bf16[2,256,512]{2,1,0:T(8,128)(2,1)S(1)} %broadcast_select_fusion), channel_id=1, source_target_pairs={{4,0},{8,4},{12,8},{16,12},{20,16},{24,20},{28,24},{0,28},{5,1},{9... | collective-permute-start | bytes 1572872 | tf_op jit(solution)/shard_map/ppermute | solution.py:11
  17.0 0.8 copy.81
  17.7 0.6 gather_fusion.1
  18.3 0.1 select_bitcast_fusion
  18.4 0.1 copy.82
  18.5 0.1 select_n.126
  18.6 0.1 select_n.124
  18.7 45.8 %all_gather.6 = bf16[16,64,192]{2,1,0:T(8,128)(2,1)S(1)} all-gather(bf16[2,64,192]{2,1,0:T(8,128)(2,1)} %param.6), channel_id=1, replica_groups=mesh['ka'=8,'col'=4] {'ka'}, dimensions={0}, use_global_device_ids=true | all-gather | bytes 442368 | tf_op jit(solution)/shard_map/all_gather | solution.py:39
  64.5 0.6 gather_fusion.2
  65.0 0.1 broadcast_select_fusion.1
  65.1 7.2 %all_gather.7 = bf16[4,256,192]{2,1,0:T(8,128)(2,1)S(1)} all-gather(bf16[4,64,192]{2,1,0:T(8,128)(2,1)S(1)} %broadcast_select_fusion.1), channel_id=1, replica_groups=mesh['ka'=8,'col'=4] {'col'}, dimensions={1}, use_global_device_ids=true | all-gather | bytes 491520 | tf_op jit(solution)/shard_map/all_gather | solution.py:41
  72.3 0.0 copy-done
  72.3 0.5 fusion
  72.8 0.1 copy.86
  72.9 1.9 broadcast_in_dim.32
  74.8 1.2 convolution_dynamic-update-slice_fusion.7
  76.0 0.0 collective-permute-done
  76.0 0.2 collective-permute-start.2
  76.2 0.0 collective-permute-done.1
  76.2 4.5 %collective-permute-start.3 = (bf16[2,256,512]{2,1,0:T(8,128)(2,1)S(1)}, bf16[2,256,512]{2,1,0:T(8,128)(2,1)S(1)}, u32[]{:S(2)}, u32[]{:S(2)}) collective-permute-start(bf16[2,256,512]{2,1,0:T(8,128)(2,1)S(1)} %collective-permute-done.1), channel_id=1, source_target_pairs={{4,0},{8,4},{12,8},{16,12},{20,16},{24,20},{28,24},{0,28},{5,1},{9... | collective-permute-start | bytes 1572872 | tf_op jit(solution)/shard_map/ppermute | solution.py:26
  80.7 1.2 convolution_dynamic-update-slice_fusion.6
  81.9 1.2 convolution_dynamic-update-slice_fusion.5
  83.1 16.1 %collective-permute-done.2 = bf16[2,256,512]{2,1,0:T(8,128)(2,1)S(1)} collective-permute-done((bf16[2,256,512]{2,1,0:T(8,128)(2,1)S(1)}, bf16[2,256,512]{2,1,0:T(8,128)(2,1)S(1)}, u32[]{:S(2)}, u32[]{:S(2)}) %collective-permute-start.2) | collective-permute-done | bytes 524320 | tf_op jit(solution)/shard_map/ppermute | solution.py:26
  99.2 2.5 %collective-permute-start.4 = (bf16[2,256,512]{2,1,0:T(8,128)(2,1)S(1)}, bf16[2,256,512]{2,1,0:T(8,128)(2,1)S(1)}, u32[]{:S(2)}, u32[]{:S(2)}) collective-permute-start(bf16[2,256,512]{2,1,0:T(8,128)(2,1)S(1)} %collective-permute-done.2), channel_id=1, source_target_pairs={{0,4},{4,8},{8,12},{12,16},{16,20},{20,24},{24,28},{28,0},{1,5},{5... | collective-permute-start | bytes 1572872 | tf_op jit(solution)/shard_map/ppermute | solution.py:26
  101.7 0.0 collective-permute-done.3
  101.7 2.7 %collective-permute-start.5 = (bf16[2,256,512]{2,1,0:T(8,128)(2,1)S(1)}, bf16[2,256,512]{2,1,0:T(8,128)(2,1)S(1)}, u32[]{:S(2)}, u32[]{:S(2)}) collective-permute-start(bf16[2,256,512]{2,1,0:T(8,128)(2,1)S(1)} %collective-permute-done.3), channel_id=1, source_target_pairs={{4,0},{8,4},{12,8},{16,12},{20,16},{24,20},{28,24},{0,28},{5,1},{9... | collective-permute-start | bytes 1572872 | tf_op jit(solution)/shard_map/ppermute | solution.py:26
  104.4 1.2 convolution_dynamic-update-slice_fusion.4
  105.6 1.2 convolution_dynamic-update-slice_fusion.3
  106.8 17.1 %collective-permute-done.4 = bf16[2,256,512]{2,1,0:T(8,128)(2,1)S(1)} collective-permute-done((bf16[2,256,512]{2,1,0:T(8,128)(2,1)S(1)}, bf16[2,256,512]{2,1,0:T(8,128)(2,1)S(1)}, u32[]{:S(2)}, u32[]{:S(2)}) %collective-permute-start.4) | collective-permute-done | bytes 524320 | tf_op jit(solution)/shard_map/ppermute | solution.py:26
  123.8 2.5 %collective-permute-start.6 = (bf16[2,256,512]{2,1,0:T(8,128)(2,1)S(1)}, bf16[2,256,512]{2,1,0:T(8,128)(2,1)S(1)}, u32[]{:S(2)}, u32[]{:S(2)}) collective-permute-start(bf16[2,256,512]{2,1,0:T(8,128)(2,1)S(1)} %collective-permute-done.4), channel_id=1, source_target_pairs={{0,4},{4,8},{8,12},{12,16},{16,20},{20,24},{24,28},{28,0},{1,5},{5... | collective-permute-start | bytes 1572872 | tf_op jit(solution)/shard_map/ppermute | solution.py:26
  126.3 1.2 convolution_dynamic-update-slice_fusion.2
  127.5 0.0 collective-permute-done.5
  127.5 1.2 convolution_dynamic-update-slice_fusion.1
  128.7 10.9 %collective-permute-done.6 = bf16[2,256,512]{2,1,0:T(8,128)(2,1)S(1)} collective-permute-done((bf16[2,256,512]{2,1,0:T(8,128)(2,1)S(1)}, bf16[2,256,512]{2,1,0:T(8,128)(2,1)S(1)}, u32[]{:S(2)}, u32[]{:S(2)}) %collective-permute-start.6) | collective-permute-done | bytes 524320 | tf_op jit(solution)/shard_map/ppermute | solution.py:26
  139.6 1.2 convolution_dynamic-update-slice_fusion
  140.8 0.0 copy-start.3
  140.8 0.0 copy-start.1
  140.8 0.0 copy-start.2
  140.8 0.0 reduce-scatter.2.cloned.1.call-update
  140.9 0.0 all-reduce.3.cloned.1.call-start
  140.9 35.8 %reduce-scatter.2.cloned.1.call-done = bf16[2,512,384]{2,1,0:T(8,128)(2,1)} async-done(((bf16[2,2048,384]{2,1,0:T(8,128)(2,1)}), bf16[2,512,384]{2,1,0:T(8,128)(2,1)}) %reduce-scatter.2.cloned.1.call-update) | async-done | bytes 786448 | tf_op jit(solution)/shard_map/reduce_scatter | solution.py:58
  176.7 1.2 convert_reduce_fusion
  177.9 0.2 copy.95
  178.1 0.3 fusion.1
  178.4 0.9 copy.96
  179.2 0.0 all-reduce.3.cloned.1.call-update
  179.3 0.0 copy-done.3
  179.3 0.6 dynamic-slice
  180.5 31.2 %all-reduce.3.cloned.1.call-done = bf16[2,256,192]{2,0,1:T(2,128)(2,1)} async-done(((bf16[2,256,192]{2,0,1:T(2,128)(2,1)}), bf16[2,256,192]{2,0,1:T(2,128)(2,1)}) %all-reduce.3.cloned.1.call-update) | async-done | bytes 196624
  211.7 0.9 constant_dynamic-slice_fusion
  212.6 0.0 copy-done.1
  212.6 0.0 copy-done.2
  212.6 0.7 multiply_add_fusion
  (6 shorter events, 0.0 us)
Async XLA Ops:
  6.5 65.8 %copy-start = (bf16[2,512,256]{2,1,0:T(8,128)(2,1)S(1)}, bf16[2,512,256]{2,1,0:T(8,128)(2,1)}, u32[]{:S(2)}) copy-start(bf16[2,512,256]{2,1,0:T(8,128)(2,1)} %param.7) | copy-start | bytes 1572868
  6.5 170.1 %reduce-scatter.2.cloned.1.call-start = ((), (), s32[]{:S(2)}) async-start(), calls=%async_computation.1 | async-start | bytes 3932160 | tf_op jit(solution)/shard_map/reduce_scatter | solution.py:58
  10.8 65.2 %collective-permute-start = (bf16[2,256,512]{2,1,0:T(8,128)(2,1)S(1)}, bf16[2,256,512]{2,1,0:T(8,128)(2,1)S(1)}, u32[]{:S(2)}, u32[]{:S(2)}) collective-permute-start(bf16[2,256,512]{2,1,0:T(8,128)(2,1)S(1)} %broadcast_select_fusion), channel_id=1, source_target_pairs={{0,4},{4,8},{8,12},{12,16},{16,20},{20,24},{24,28},{28,0},{1,5},{5... | collective-permute-start | bytes 1572872 | tf_op jit(solution)/shard_map/ppermute | solution.py:11
  13.9 62.4 %collective-permute-start.1 = (bf16[2,256,512]{2,1,0:T(8,128)(2,1)S(1)}, bf16[2,256,512]{2,1,0:T(8,128)(2,1)S(1)}, u32[]{:S(2)}, u32[]{:S(2)}) collective-permute-start(bf16[2,256,512]{2,1,0:T(8,128)(2,1)S(1)} %broadcast_select_fusion), channel_id=1, source_target_pairs={{4,0},{8,4},{12,8},{16,12},{20,16},{24,20},{28,24},{0,28},{5,1},{9... | collective-permute-start | bytes 1572872 | tf_op jit(solution)/shard_map/ppermute | solution.py:11
  76.0 23.2 %collective-permute-start.2 = (bf16[2,256,512]{2,1,0:T(8,128)(2,1)S(1)}, bf16[2,256,512]{2,1,0:T(8,128)(2,1)S(1)}, u32[]{:S(2)}, u32[]{:S(2)}) collective-permute-start(bf16[2,256,512]{2,1,0:T(8,128)(2,1)S(1)} %collective-permute-done), channel_id=1, source_target_pairs={{0,4},{4,8},{8,12},{12,16},{16,20},{20,24},{24,28},{28,0},{1,5},{5... | collective-permute-start | bytes 1572872 | tf_op jit(solution)/shard_map/ppermute | solution.py:26
  76.2 25.5 %collective-permute-start.3 = (bf16[2,256,512]{2,1,0:T(8,128)(2,1)S(1)}, bf16[2,256,512]{2,1,0:T(8,128)(2,1)S(1)}, u32[]{:S(2)}, u32[]{:S(2)}) collective-permute-start(bf16[2,256,512]{2,1,0:T(8,128)(2,1)S(1)} %collective-permute-done.1), channel_id=1, source_target_pairs={{4,0},{8,4},{12,8},{16,12},{20,16},{24,20},{28,24},{0,28},{5,1},{9... | collective-permute-start | bytes 1572872 | tf_op jit(solution)/shard_map/ppermute | solution.py:26
  99.2 24.6 %collective-permute-start.4 = (bf16[2,256,512]{2,1,0:T(8,128)(2,1)S(1)}, bf16[2,256,512]{2,1,0:T(8,128)(2,1)S(1)}, u32[]{:S(2)}, u32[]{:S(2)}) collective-permute-start(bf16[2,256,512]{2,1,0:T(8,128)(2,1)S(1)} %collective-permute-done.2), channel_id=1, source_target_pairs={{0,4},{4,8},{8,12},{12,16},{16,20},{20,24},{24,28},{28,0},{1,5},{5... | collective-permute-start | bytes 1572872 | tf_op jit(solution)/shard_map/ppermute | solution.py:26
  101.7 25.8 %collective-permute-start.5 = (bf16[2,256,512]{2,1,0:T(8,128)(2,1)S(1)}, bf16[2,256,512]{2,1,0:T(8,128)(2,1)S(1)}, u32[]{:S(2)}, u32[]{:S(2)}) collective-permute-start(bf16[2,256,512]{2,1,0:T(8,128)(2,1)S(1)} %collective-permute-done.3), channel_id=1, source_target_pairs={{4,0},{8,4},{12,8},{16,12},{20,16},{24,20},{28,24},{0,28},{5,1},{9... | collective-permute-start | bytes 1572872 | tf_op jit(solution)/shard_map/ppermute | solution.py:26
  123.8 15.8 %collective-permute-start.6 = (bf16[2,256,512]{2,1,0:T(8,128)(2,1)S(1)}, bf16[2,256,512]{2,1,0:T(8,128)(2,1)S(1)}, u32[]{:S(2)}, u32[]{:S(2)}) collective-permute-start(bf16[2,256,512]{2,1,0:T(8,128)(2,1)S(1)} %collective-permute-done.4), channel_id=1, source_target_pairs={{0,4},{4,8},{8,12},{12,16},{16,20},{20,24},{24,28},{28,0},{1,5},{5... | collective-permute-start | bytes 1572872 | tf_op jit(solution)/shard_map/ppermute | solution.py:26
  140.8 38.5 %copy-start.3 = (u32[32]{0:T(128)S(1)}, u32[32]{0:T(128)}, u32[]{:S(2)}) copy-start(u32[32]{0:T(128)} %constant.111) | copy-start | bytes 388
  140.8 71.8 %copy-start.1 = (bf16[2,64,192]{2,1,0:T(8,128)(2,1)S(1)}, bf16[2,64,192]{2,1,0:T(8,128)(2,1)}, u32[]{:S(2)}) copy-start(bf16[2,64,192]{2,1,0:T(8,128)(2,1)} %param.6) | copy-start | bytes 147460
  140.8 71.8 %copy-start.2 = (f32[2,64]{1,0:T(2,128)S(1)}, f32[2,64]{1,0:T(2,128)}, u32[]{:S(2)}) copy-start(f32[2,64]{1,0:T(2,128)} %param.9) | copy-start | bytes 1540
  140.9 70.8 %all-reduce.3.cloned.1.call-start = ((), (), s32[]{:S(2)}) async-start(), calls=%async_computation.2 | async-start | bytes 524288
Sparse Core Ops, SparseCore 0:
  141.0 35.6 reduce-scatter.1
  179.4 32.2 all-reduce.2
